TPU v7x, 32 devices: a whole 2x2x4 slice. The times are simulated.
32 devices in a mesh: groups: 2 (over y), dp: 4 (over z), seq: 4 (over x, core).
Axes of the slice: x: 2, y: 2, z: 4, core: 2. Of those that a mesh axis runs over, the one named last changes fastest.
Arguments:
- query_rows: bfloat16 [8, 1024, 8192], P(('groups', 'dp'), 'seq'), parts along dimension 0, may hold values from -60 to 60
- key_rows: bfloat16 [8, 1024, 1024], P(('groups', 'dp'), 'seq'), parts along dimension 0, may hold values from -4 to 4
- placed_value_rows: bfloat16 [8, 1024, 1024], P(('groups', 'dp'), 'seq'), parts along dimension 0, may hold values from -4 to 4
- doc_lengths: int32 [8, 8], P(('groups', 'dp')), parts along dimension 0, may hold values from 1 to 512, 1024 in all within a row
- span_order: int32 [8, 8], P(('groups', 'dp')), parts along dimension 0, may hold values from 0 to 7, each once within a row
- out_weight: bfloat16 [8192, 8192], P('dp', 'seq'), may hold values from -0.25 to 0.25
Outputs:
- whitened: float32 [32, 512, 8192], P(('groups', 'seq'), None, 'dp'), parts along dimension 0
There are 2 independent parts, one for each index of `groups`. A program takes and returns all parts, laid end to end along the dimension named above; an argument that names none is the same for every part. Nothing has to cross between parts.
All inputs are finite; a program needn't handle non-finite values.
Results may differ from a plain program's by a relative error of at most 0.00073.
Values may be sent and summed in bfloat16 or wider, within the bound.
A program may use at most 128 MiB of HBM per device.

v0:
```python
import jax
import jax.numpy as jnp
from jax import lax
from jax.sharding import PartitionSpec as P

QUERY_HEADS = 64
KEY_VALUE_HEADS = 8
HEAD_SIZE = 128
BLOCK_W = 512
NB = 16


def doc_numbers(positions, lengths):
    starts = jnp.cumsum(lengths) - lengths
    return jnp.sum((positions[:, None] >= starts[None, :]).astype(jnp.int32), axis=1)


def local_attention(query_local, key_all, value_all, visible):
    tok_count = query_local.shape[0]
    head_group = QUERY_HEADS // KEY_VALUE_HEADS
    results = []
    for kv_index in range(KEY_VALUE_HEADS):
        key_head = key_all[:, kv_index * HEAD_SIZE : (kv_index + 1) * HEAD_SIZE]
        value_head = value_all[:, kv_index * HEAD_SIZE : (kv_index + 1) * HEAD_SIZE]
        query_group = query_local[
            :, kv_index * head_group * HEAD_SIZE : (kv_index + 1) * head_group * HEAD_SIZE
        ].reshape(tok_count, head_group, HEAD_SIZE)
        scores = jnp.einsum(
            "qgd,kd->gqk", query_group, key_head, preferred_element_type=jnp.float32
        ) * HEAD_SIZE ** (-0.5)
        scores = jnp.where(visible[None], scores, -1e30)
        largest = jnp.max(scores, axis=2, keepdims=True)
        lifted = jnp.exp(scores - largest)
        weights = (lifted / jnp.sum(lifted, axis=2, keepdims=True)).astype(jnp.bfloat16)
        mixed = jnp.einsum("gqk,kd->qgd", weights, value_head, preferred_element_type=jnp.float32)
        results.append(mixed.reshape(tok_count, head_group * HEAD_SIZE))
    return jnp.concatenate(results, axis=1)


def block_outer(blocks):
    return jnp.einsum("rbi,rbj->bij", blocks, blocks, precision=lax.Precision.HIGHEST)


def shards(query_rows, key_rows, placed_value_rows, doc_lengths, span_order, out_weight):
    tok_count = query_rows.shape[1]
    seq_count = lax.axis_size("seq")
    seq_length = tok_count * seq_count
    span_rows = tok_count // 2
    lengths = doc_lengths[0]
    placement = span_order[0]
    query_local = query_rows[0]
    key_local = key_rows[0]
    value_local = placed_value_rows[0]
    key_all, value_all = (
        lax.all_gather(key_local, "seq", axis=0, tiled=True),
        lax.all_gather(value_local, "seq", axis=0, tiled=True),
    )
    row_ids = jnp.arange(seq_length, dtype=jnp.int32)
    positions = placement[row_ids // span_rows] * span_rows + row_ids % span_rows
    doc_ids = doc_numbers(positions, lengths)
    own_start = lax.axis_index("seq") * tok_count
    query_pos = lax.dynamic_slice_in_dim(positions, own_start, tok_count, 0)
    query_docs = lax.dynamic_slice_in_dim(doc_ids, own_start, tok_count, 0)
    visible = (query_docs[:, None] == doc_ids[None, :]) & (positions[None, :] <= query_pos[:, None])
    outputs = local_attention(query_local, key_all, value_all, visible)
    blocks = outputs.reshape(tok_count, NB, BLOCK_W)
    grams = lax.psum_scatter(block_outer(blocks), "seq", scatter_dimension=0, tiled=True)
    block_count = grams.shape[0]
    traces = jnp.trace(grams, axis1=1, axis2=2)
    identity = jnp.eye(BLOCK_W, dtype=jnp.float32)
    damped = grams + (0.1 * traces / BLOCK_W)[:, None, None] * identity
    summed = lax.psum(damped, "dp")
    upper = jnp.swapaxes(jnp.linalg.cholesky(summed), 1, 2)
    weight_blocks = out_weight.astype(jnp.float32).reshape(
        out_weight.shape[0], block_count, BLOCK_W
    )
    return jnp.einsum("bij,obj->bio", upper, weight_blocks, precision=lax.Precision.HIGHEST)


def solution(mesh):
    in_specs = (
        P(("groups", "dp"), "seq", None),
        P(("groups", "dp"), "seq", None),
        P(("groups", "dp"), "seq", None),
        P(("groups", "dp"), None),
        P(("groups", "dp"), None),
        P("dp", "seq"),
    )
    out_specs = P(("groups", "seq"), None, "dp")
    return jax.shard_map(shards, mesh=mesh, in_specs=in_specs, out_specs=out_specs, check_vma=False)
```

profile of v0, /device:TPU:0, one launch (start us, length us, event | category | flops | bytes accessed | tf_op | source)
XLA Modules:
  0.0 871.1 jit_solution(3621411485237233564)
XLA Ops:
  17.9 6.4 copy.92
  28.6 5.6 all-gather.5.cloned.1.call-done
  34.2 7.1 fusion.119
  41.3 17.3 %all-gather.7.cloned.1.call-done = bf16[1,1024,1024]{1,2,0:T(8,128)(2,1)} async-done(((bf16[1,256,1024]{1,2,0:T(8,128)(2,1)}), bf16[1,1024,1024]{1,2,0:T(8,128)(2,1)}) %all-gather.7.cloned.1.call-update) | async-done | bytes 2097168 | tf_op jit(solution)/shard_map/all_gather | solution.py:56
  63.2 7.1 fusion.118
  75.9 7.3 fusion.120
  87.8 20.7 %fusion.121 = (f32[8,256]{1,0:T(8,128)S(1)}, f32[8,256,1024]{1,2,0:T(8,128)}) fusion(pred[256,1024]{0,1:T(8,128)(4,1)S(1)} %compare_and_fusion, bf16[256,8,128]{0,2,1:T(8,128)(2,1)} %bitcast.316, bf16[1024,1024]{1,0:T(8,128)(2,1)} %bitcast.324), kind=kOutput, calls=%fused_computation.208 | convolution fusion | flops 545260544 | bytes 9445376 | tf_op jit(solution)/shard_map/sub | solution.py:33
  108.4 5.3 fusion.49
  115.3 7.3 fusion.122
  130.4 7.3 fusion.123
  145.4 7.3 fusion.124
  160.5 7.3 fusion.125
  184.2 35.3 %fusion.126 = f32[16,512,512]{1,2,0:T(8,128)} fusion(f32[256,16,512]{2,0,1:T(8,128)} %constant_dynamic-update-slice_fusion), kind=kOutput, calls=%fused_computation.213 | convolution fusion | flops 12884901888 | bytes 25165824 | tf_op jit(solution)/shard_map/rbi,rbj->bij/dot_general | solution.py:41
  219.8 124.9 %reduce-scatter.2.cloned.1.call-done = f32[4,512,512]{1,2,0:T(8,128)} async-done(((f32[16,512,512]{1,2,0:T(8,128)}), f32[4,512,512]{1,2,0:T(8,128)}) %reduce-scatter.2.cloned.1.call-update) | async-done | bytes 4194320 | tf_op jit(solution)/shard_map/reduce_scatter | solution.py:67
  352.8 155.0 %all-reduce.3.cloned.1.call-done = f32[4,512,512]{1,2,0:T(8,128)} async-done(((f32[4,512,512]{1,2,0:T(8,128)}), f32[4,512,512]{1,2,0:T(8,128)}) %all-reduce.3.cloned.1.call-update) | async-done | bytes 4194320 | tf_op jit(solution)/shard_map/psum | solution.py:72
  507.8 5.2 copy.120
  519.6 46.9 %custom-call.31 = f32[4,128,128]{2,1,0:T(8,128)S(1)} custom-call(f32[4,128,128]{2,1,0:T(8,128)S(1)} %cholesky.271), custom_call_target="Cholesky" | custom-call | tf_op jit(solution)/shard_map/jit(cholesky)/cholesky | solution.py:73
  566.5 39.3 %custom-call.32 = f32[4,1,128,128]{2,3,1,0:T(8,128)S(1)} custom-call(f32[4,1,128,128]{3,2,1,0:T(8,128)S(1)} %select_bitcast_fusion.2), custom_call_target="InvertDiagBlocksLowerTriangular" | custom-call | tf_op jit(solution)/shard_map/jit(cholesky)/cholesky | solution.py:73
  610.3 47.1 %custom-call.33 = f32[4,128,128]{2,1,0:T(8,128)S(1)} custom-call(f32[4,128,128]{2,1,0:T(8,128)S(1)} %cholesky.275), custom_call_target="Cholesky" | custom-call | tf_op jit(solution)/shard_map/jit(cholesky)/cholesky | solution.py:73
  657.5 39.3 %custom-call.34 = f32[4,1,128,128]{2,3,1,0:T(8,128)S(1)} custom-call(f32[4,1,128,128]{3,2,1,0:T(8,128)S(1)} %select_bitcast_fusion.1), custom_call_target="InvertDiagBlocksLowerTriangular" | custom-call | tf_op jit(solution)/shard_map/jit(cholesky)/cholesky | solution.py:73
  703.1 47.3 %custom-call.35 = f32[4,128,128]{2,1,0:T(8,128)S(1)} custom-call(f32[4,128,128]{2,1,0:T(8,128)S(1)} %cholesky.280), custom_call_target="Cholesky" | custom-call | tf_op jit(solution)/shard_map/jit(cholesky)/cholesky | solution.py:73
  751.3 39.3 %custom-call.36 = f32[4,1,128,128]{2,3,1,0:T(8,128)S(1)} custom-call(f32[4,1,128,128]{3,2,1,0:T(8,128)S(1)} %select_bitcast_fusion), custom_call_target="InvertDiagBlocksLowerTriangular" | custom-call | tf_op jit(solution)/shard_map/jit(cholesky)/cholesky | solution.py:73
  795.0 47.1 %custom-call.37 = f32[4,128,128]{2,1,0:T(8,128)S(1)} custom-call(f32[4,128,128]{2,1,0:T(8,128)S(1)} %convolution_subtract_fusion.2), custom_call_target="Cholesky" | custom-call | tf_op jit(solution)/shard_map/jit(cholesky)/cholesky | solution.py:73
  843.4 21.0 %fusion.8 = f32[4,512,2048]{2,1,0:T(8,128)} fusion(bf16[256,4,8,512]{3,2,1,0:T(8,128)(2,1)} %bitcast.302, f32[4,512,512]{1,2,0:T(8,128)} %constant_dynamic-update-slice_fusion.8, pred[4]{0:T(512)(128)(4,1)S(1)} %or_or_fusion, pred[512,512]{0,1:T(8,128)(4,1)S(1)} %iota_compare_fusion.1), kind=kOutput, calls=%fused_computation.8 | convolution fusion | flops 25771900928 | bytes 29622276 | tf_op jit(solution)/shard_map/bij,obj->bio/dot_general | solution.py:77
  (88 shorter events, 103.5 us)
Async XLA Ops:
  6.5 27.7 %all-gather.5.cloned.1.call-start = ((), (), s32[]{:S(2)}) async-start(), calls=%async_computation.3 | async-start | bytes 2621440 | tf_op jit(solution)/shard_map/all_gather | solution.py:55
  7.3 51.3 %all-gather.7.cloned.1.call-start = ((), (), s32[]{:S(2)}) async-start(), calls=%async_computation.4 | async-start | bytes 2621440 | tf_op jit(solution)/shard_map/all_gather | solution.py:56
  9.4 335.4 %reduce-scatter.2.cloned.1.call-start = ((), (), s32[]{:S(2)}) async-start(), calls=%async_computation.1 | async-start | bytes 20971520 | tf_op jit(solution)/shard_map/reduce_scatter | solution.py:67
  175.5 5.5 copy-start.2
  175.5 6.6 copy-start.3
  175.5 7.6 copy-start.4
  219.6 288.3 %all-reduce.3.cloned.1.call-start = ((), (), s32[]{:S(2)}) async-start(), calls=%async_computation.2 | async-start | bytes 8388608 | tf_op jit(solution)/shard_map/psum | solution.py:72
  517.6 2.0 copy-start.1
  698.2 1.9 copy-start
Sparse Core Ops, SparseCore 0:
  8.9 25.2 all-gather.4
  35.8 22.8 all-gather.6
  219.7 125.0 reduce-scatter.1
  352.8 154.9 all-reduce.2
where the time goes:
time: 881 us; the launch traced here: 871 us
  other arithmetic  326 us (37%)
  waiting for transfers between devices  304 us (35%)
  matrix products  178 us (20%)
  local copies, waits for them, and re-layouts  48.8 us (6%)
  between operations  13.7 us (2%)
    another operation x16, other arithmetic, shards(): upper = jnp.swapaxes(jnp.linalg.cholesky(summed), 1, 2)  307 us
    psum x1, waiting for transfers between devices, shards(): summed = lax.psum(damped, 'dp')  155 us
    reduce_scatter x1, waiting for transfers between devices, shards(): lax.psum_scatter(block_outer(blocks), 'seq', scatter_dimension=0, tiled=T...  125 us
    sub x8, matrix products, local_attention(): lifted = jnp.exp(scores - largest)  71.6 us
    dot_general x8, matrix products, local_attention(): jnp.einsum('gqk,kd->qgd', weights, value_head, preferred_element_type=jnp...  38.6 us
    dot_general x1, matrix products, block_outer(): jnp.einsum('rbi,rbj->bij', blocks, blocks, precision=lax.Precision.HIGHEST)  35.3 us
    unnamed x19, local copies, waits for them, and re-layouts  21.1 us
    dot_general x1, matrix products, shards(): jnp.einsum('bij,obj->bio', upper, weight_blocks, precision=lax.Precision....  21 us
  transfers between devices with their start and end apart: 4, of which 4 were waited for; matrix products, arithmetic and copies ran while one was open for 3% of the time, Pallas kernels for 0%

commit v1 on v0

--- a/solution.py
+++ b/solution.py
@@ -69,7 +69,9 @@
     traces = jnp.trace(grams, axis1=1, axis2=2)
     identity = jnp.eye(BLOCK_W, dtype=jnp.float32)
     damped = grams + (0.1 * traces / BLOCK_W)[:, None, None] * identity
-    summed = lax.psum(damped, "dp")
+    summed = damped
+    for hop in (1, 2):
+        summed = summed + lax.ppermute(summed, "dp", [(dev, dev ^ hop) for dev in range(4)])
     upper = jnp.swapaxes(jnp.linalg.cholesky(summed), 1, 2)
     weight_blocks = out_weight.astype(jnp.float32).reshape(
         out_weight.shape[0], block_count, BLOCK_W

time: 881 us -> 999 us (1.13)
  waiting for transfers between devices: 304 us -> 419 us
    ppermute x0 -> x2, waiting for transfers between devices: none -> 270 us  [shards(): lax.ppermute(summed, 'dp', [(dev, dev ^ hop) for dev in range(4)])]
    psum x1 -> x0, waiting for transfers between devices: 155 us -> none  [shards(): summed = lax.psum(damped, 'dp')]
    sub x8, matrix products: 71.6 us -> 58.5 us  [local_attention(): lifted = jnp.exp(scores - largest)]
    unnamed x19 -> x21, local copies, waits for them, and re-layouts: 21.1 us -> 21.1 us
  transfers between devices with their start and end apart: 4 -> 5, of which waited for: 4 -> 5; matrix products, arithmetic and copies ran while one was open for 3% -> 3% of each run, Pallas kernels for 0% -> 0%
where the time goes in v1:
time: 999 us; the launch traced here: 989 us
  waiting for transfers between devices  419 us (42%)
  other arithmetic  329 us (33%)
  matrix products  175 us (18%)
  local copies, waits for them, and re-layouts  48.8 us (5%)
  between operations  13.9 us (1%)
    another operation x16, other arithmetic, shards(): upper = jnp.swapaxes(jnp.linalg.cholesky(summed), 1, 2)  307 us
    ppermute x2, waiting for transfers between devices, shards(): lax.ppermute(summed, 'dp', [(dev, dev ^ hop) for dev in range(4)])  270 us
    reduce_scatter x1, waiting for transfers between devices, shards(): lax.psum_scatter(block_outer(blocks), 'seq', scatter_dimension=0, tiled=T...  125 us
    sub x8, matrix products, local_attention(): lifted = jnp.exp(scores - largest)  58.5 us
    dot_general x1, matrix products, block_outer(): jnp.einsum('rbi,rbj->bij', blocks, blocks, precision=lax.Precision.HIGHEST)  44.8 us
    dot_general x8, matrix products, local_attention(): jnp.einsum('gqk,kd->qgd', weights, value_head, preferred_element_type=jnp...  38.6 us
    unnamed x21, local copies, waits for them, and re-layouts  21.1 us
    dot_general x1, matrix products, shards(): jnp.einsum('bij,obj->bio', upper, weight_blocks, precision=lax.Precision....  21 us
  transfers between devices with their start and end apart: 5, of which 5 were waited for; matrix products, arithmetic and copies ran while one was open for 3% of the time, Pallas kernels for 0%

profile of v1, /device:TPU:0, one launch (start us, length us, event | category | flops | bytes accessed | tf_op | source)
XLA Modules:
  0.0 989.2 jit_solution(9972795822654558003)
XLA Ops:
  17.9 6.4 copy.92
  28.6 5.6 all-gather.5.cloned.1.call-done
  34.2 7.1 fusion.124
  41.3 17.3 %all-gather.7.cloned.1.call-done = bf16[1,1024,1024]{1,2,0:T(8,128)(2,1)} async-done(((bf16[1,256,1024]{1,2,0:T(8,128)(2,1)}), bf16[1,1024,1024]{1,2,0:T(8,128)(2,1)}) %all-gather.7.cloned.1.call-update) | async-done | bytes 2097168 | tf_op jit(solution)/shard_map/all_gather | solution.py:56
  63.2 7.1 fusion.123
  75.9 7.3 fusion.125
  87.8 7.6 fusion.126
  95.4 5.3 fusion.49
  102.2 7.3 fusion.127
  117.3 7.3 fusion.128
  132.3 7.3 fusion.129
  147.4 7.3 fusion.130
  171.2 44.8 %fusion.131 = f32[16,512,512]{1,2,0:T(8,128)} fusion(f32[256,16,512]{2,0,1:T(8,128)} %constant_dynamic-update-slice_fusion), kind=kOutput, calls=%fused_computation.216 | convolution fusion | flops 12884901888 | bytes 25165824 | tf_op jit(solution)/shard_map/rbi,rbj->bij/dot_general | solution.py:41
  216.2 125.0 %reduce-scatter.2.cloned.1.call-done = f32[4,512,512]{1,2,0:T(8,128)} async-done(((f32[16,512,512]{1,2,0:T(8,128)}), f32[4,512,512]{1,2,0:T(8,128)}) %reduce-scatter.2.cloned.1.call-update) | async-done | bytes 4194320 | tf_op jit(solution)/shard_map/reduce_scatter | solution.py:67
  348.8 90.7 %collective-permute-done = f32[4,512,512]{1,2,0:T(8,128)S(1)} collective-permute-done((f32[4,512,512]{1,2,0:T(8,128)S(1)}, f32[4,512,512]{1,2,0:T(8,128)S(1)}, u32[]{:S(2)}, u32[]{:S(2)}) %collective-permute-start) | collective-permute-done | bytes 4194336 | tf_op jit(solution)/shard_map/ppermute | solution.py:74
  443.3 179.5 %collective-permute-done.1 = f32[4,512,512]{1,2,0:T(8,128)S(1)} collective-permute-done((f32[4,512,512]{1,2,0:T(8,128)S(1)}, f32[4,512,512]{1,2,0:T(8,128)S(1)}, u32[]{:S(2)}, u32[]{:S(2)}) %collective-permute-start.1) | collective-permute-done | bytes 4194336 | tf_op jit(solution)/shard_map/ppermute | solution.py:74
  637.6 46.9 %custom-call.31 = f32[4,128,128]{2,1,0:T(8,128)S(1)} custom-call(f32[4,128,128]{2,1,0:T(8,128)S(1)} %cholesky.271), custom_call_target="Cholesky" | custom-call | tf_op jit(solution)/shard_map/jit(cholesky)/cholesky | solution.py:75
  684.6 39.5 %custom-call.32 = f32[4,1,128,128]{2,3,1,0:T(8,128)S(1)} custom-call(f32[4,1,128,128]{3,2,1,0:T(8,128)S(1)} %select_bitcast_fusion.2), custom_call_target="InvertDiagBlocksLowerTriangular" | custom-call | tf_op jit(solution)/shard_map/jit(cholesky)/cholesky | solution.py:75
  728.5 46.9 %custom-call.33 = f32[4,128,128]{2,1,0:T(8,128)S(1)} custom-call(f32[4,128,128]{2,1,0:T(8,128)S(1)} %cholesky.275), custom_call_target="Cholesky" | custom-call | tf_op jit(solution)/shard_map/jit(cholesky)/cholesky | solution.py:75
  775.5 39.3 %custom-call.34 = f32[4,1,128,128]{2,3,1,0:T(8,128)S(1)} custom-call(f32[4,1,128,128]{3,2,1,0:T(8,128)S(1)} %select_bitcast_fusion.1), custom_call_target="InvertDiagBlocksLowerTriangular" | custom-call | tf_op jit(solution)/shard_map/jit(cholesky)/cholesky | solution.py:75
  821.1 47.1 %custom-call.35 = f32[4,128,128]{2,1,0:T(8,128)S(1)} custom-call(f32[4,128,128]{2,1,0:T(8,128)S(1)} %cholesky.280), custom_call_target="Cholesky" | custom-call | tf_op jit(solution)/shard_map/jit(cholesky)/cholesky | solution.py:75
  869.1 39.3 %custom-call.36 = f32[4,1,128,128]{2,3,1,0:T(8,128)S(1)} custom-call(f32[4,1,128,128]{3,2,1,0:T(8,128)S(1)} %select_bitcast_fusion), custom_call_target="InvertDiagBlocksLowerTriangular" | custom-call | tf_op jit(solution)/shard_map/jit(cholesky)/cholesky | solution.py:75
  912.8 47.1 %custom-call.37 = f32[4,128,128]{2,1,0:T(8,128)S(1)} custom-call(f32[4,128,128]{2,1,0:T(8,128)S(1)} %slice_subtract_fusion.2), custom_call_target="Cholesky" | custom-call | tf_op jit(solution)/shard_map/jit(cholesky)/cholesky | solution.py:75
  961.2 21.0 %fusion.8 = f32[4,512,2048]{2,1,0:T(8,128)} fusion(bf16[256,4,8,512]{3,2,1,0:T(8,128)(2,1)} %bitcast.302, f32[4,512,512]{1,2,0:T(8,128)} %constant_dynamic-update-slice_fusion.8, pred[4]{0:T(512)(128)(4,1)S(1)} %or_or_fusion, pred[512,512]{0,1:T(8,128)(4,1)S(1)} %iota_compare_fusion.1), kind=kOutput, calls=%fused_computation.8 | convolution fusion | flops 25771900928 | bytes 29622276 | tf_op jit(solution)/shard_map/bij,obj->bio/dot_general | solution.py:79
  (93 shorter events, 115.1 us)
Async XLA Ops:
  6.5 27.7 %all-gather.5.cloned.1.call-start = ((), (), s32[]{:S(2)}) async-start(), calls=%async_computation.2 | async-start | bytes 2621440 | tf_op jit(solution)/shard_map/all_gather | solution.py:55
  7.3 51.3 %all-gather.7.cloned.1.call-start = ((), (), s32[]{:S(2)}) async-start(), calls=%async_computation.3 | async-start | bytes 2621440 | tf_op jit(solution)/shard_map/all_gather | solution.py:56
  9.4 331.8 %reduce-scatter.2.cloned.1.call-start = ((), (), s32[]{:S(2)}) async-start(), calls=%async_computation.1 | async-start | bytes 20971520 | tf_op jit(solution)/shard_map/reduce_scatter | solution.py:67
  162.5 5.5 copy-start.3
  162.5 6.6 copy-start.4
  162.5 7.6 copy-start.5
  341.2 98.2 %copy-start.1 = (f32[4,512,512]{1,2,0:T(8,128)S(1)}, f32[4,512,512]{1,2,0:T(8,128)}, u32[]{:S(2)}) copy-start(f32[4,512,512]{1,2,0:T(8,128)} %reduce-scatter.2.cloned.1.call-done) | copy-start | bytes 12582916
  347.2 92.2 %collective-permute-start = (f32[4,512,512]{1,2,0:T(8,128)S(1)}, f32[4,512,512]{1,2,0:T(8,128)S(1)}, u32[]{:S(2)}, u32[]{:S(2)}) collective-permute-start(f32[4,512,512]{1,2,0:T(8,128)S(1)} %multiply_add_fusion), channel_id=1, source_target_pairs={{0,4},{4,0},{8,12},{12,8},{1,5},{5,1},{9,13},{13,9},{2,6},{6,2},{1... | collective-permute-start | bytes 12582920 | tf_op jit(solution)/shard_map/ppermute | solution.py:74
  440.7 182.1 %collective-permute-start.1 = (f32[4,512,512]{1,2,0:T(8,128)S(1)}, f32[4,512,512]{1,2,0:T(8,128)S(1)}, u32[]{:S(2)}, u32[]{:S(2)}) collective-permute-start(f32[4,512,512]{1,2,0:T(8,128)S(1)} %fusion.151), channel_id=1, source_target_pairs={{0,8},{4,12},{8,0},{12,4},{1,9},{5,13},{9,1},{13,5},{2,10},{6,14},... | collective-permute-start | bytes 12582920 | tf_op jit(solution)/shard_map/ppermute | solution.py:74
  635.6 2.0 copy-start.2
  816.2 1.9 copy-start
Sparse Core Ops, SparseCore 0:
  8.9 25.2 all-gather.4
  35.8 22.8 all-gather.6
  216.1 125.0 reduce-scatter.1
